TPU v7x, 256 devices: a whole 4x4x8 slice. The times are simulated.
256 devices in a mesh: ctx: 32 (over x_hi, z, core), tp: 8 (over x_lo, y).
Axes of the slice: x: 4 (x_hi: 2, x_lo: 2; x = x_hi * 2 + x_lo), y: 4, z: 8, core: 2. Of those that a mesh axis runs over, the one named last changes fastest.
Arguments:
- features: bfloat16 [3, 4096, 8192], P(None, 'ctx', 'tp'), may hold values from -6 to 6
- conv_weight: float32 [3, 3, 8192], replicated, may hold values from -3 to 3
- decay_rates: float32 [16, 8192], P(None, ('tp', 'ctx')), may hold values from 1e-05 to 0.03
- residues: float32 [16, 8192], P(None, ('tp', 'ctx')), may hold values from -1.5 to 1.5
- skip_gain: float32 [8192], P(('tp', 'ctx')), may hold values from -1 to 1
- out_weight: bfloat16 [8192, 8192], P('tp', 'ctx'), may hold values from -0.0625 to 0.0625
Outputs:
- mixed: bfloat16 [4096, 8192], P('ctx', 'tp')
All inputs are finite; a program needn't handle non-finite values.
Results may differ from a plain program's by a relative error of at most 0.014.
Values may be sent and summed in bfloat16 or wider, within the bound.
A program may use at most 64 MiB of HBM per device.

v0:
```python
import math
import jax
import jax.numpy as jnp
from jax import lax
from jax.sharding import PartitionSpec as P


def shifted(shard, axis, by):
    count = lax.axis_size(axis)
    pairs = [(i, i + by) for i in range(count) if 0 <= i + by < count]
    return lax.ppermute(shard, axis, pairs)


def angle_table(first, second, modulus):
    left = jnp.arange(first, dtype=jnp.int32)[:, None]
    right = jnp.arange(second, dtype=jnp.int32)[None, :]
    return (left * right % modulus).astype(jnp.float32) * (2.0 * math.pi / modulus)


def grid_sizes(length):
    total = 2 * length
    rows = math.gcd(total, 128)
    return (total, rows, total // rows)


def forward_dft(signal):
    count, length = signal.shape
    total, rows, cols = grid_sizes(length)
    half = rows // 2
    exact = lax.Precision.HIGH
    grid = signal.reshape(count, half, cols)
    first = angle_table(half, rows, rows)
    part_re = jnp.einsum("cab,ak->cbk", grid, jnp.cos(first), precision=exact)
    part_im = -jnp.einsum("cab,ak->cbk", grid, jnp.sin(first), precision=exact)
    twist = angle_table(cols, rows, total)
    twist_cos = jnp.cos(twist)
    twist_sin = jnp.sin(twist)
    turned_re = part_re * twist_cos + part_im * twist_sin
    turned_im = part_im * twist_cos - part_re * twist_sin
    second = angle_table(cols, cols, cols)
    second_cos = jnp.cos(second)
    second_sin = jnp.sin(second)
    out_re = jnp.einsum("cbk,bj->ckj", turned_re, second_cos, precision=exact) + jnp.einsum(
        "cbk,bj->ckj", turned_im, second_sin, precision=exact
    )
    out_im = jnp.einsum("cbk,bj->ckj", turned_im, second_cos, precision=exact) - jnp.einsum(
        "cbk,bj->ckj", turned_re, second_sin, precision=exact
    )
    return (out_re, out_im)


def inverse_dft(spec_re, spec_im, length):
    count = spec_re.shape[0]
    total, rows, cols = grid_sizes(length)
    half = rows // 2
    exact = lax.Precision.HIGH
    third = angle_table(cols, cols, cols)
    third_cos = jnp.cos(third)
    third_sin = jnp.sin(third)
    step_re = jnp.einsum("ckj,jb->ckb", spec_re, third_cos, precision=exact) - jnp.einsum(
        "ckj,jb->ckb", spec_im, third_sin, precision=exact
    )
    step_im = jnp.einsum("ckj,jb->ckb", spec_re, third_sin, precision=exact) + jnp.einsum(
        "ckj,jb->ckb", spec_im, third_cos, precision=exact
    )
    twist = angle_table(rows, cols, total)
    twist_cos = jnp.cos(twist)
    twist_sin = jnp.sin(twist)
    turned_re = step_re * twist_cos - step_im * twist_sin
    turned_im = step_re * twist_sin + step_im * twist_cos
    last = angle_table(rows, half, rows)
    result = jnp.einsum("ckb,ka->cab", turned_re, jnp.cos(last), precision=exact) - jnp.einsum(
        "ckb,ka->cab", turned_im, jnp.sin(last), precision=exact
    )
    return result.reshape(count, half * cols) / total


def long_filter(rates_local, residues_local, length):
    steps_axis = jnp.arange(length, dtype=jnp.float32)

    def add_mode(mode_index, total):
        rate_now = rates_local[mode_index][:, None]
        weight_now = residues_local[mode_index][:, None]
        return total + weight_now * jnp.sqrt(2.0 * rate_now) * jnp.exp(-rate_now * steps_axis)

    start = jnp.zeros((rates_local.shape[1], length), jnp.float32)
    return lax.fori_loop(0, rates_local.shape[0], add_mode, start)


def per_device(features, conv_weight, decay_rates, residues, skip_gain, out_weight):
    tok_rows = features.shape[1]
    width_local = features.shape[2]
    last_rows = features[:, tok_rows - 2 :, :]
    previous = shifted(last_rows, "ctx", 1)
    extended = jnp.concatenate([previous, features], axis=1).astype(jnp.float32)
    taps = conv_weight[:, :, :, None].transpose(0, 1, 3, 2)
    tp_start = lax.axis_index("tp") * width_local
    taps = lax.dynamic_slice_in_dim(taps, tp_start, width_local, 3)
    filtered = (
        taps[:, 0] * extended[:, 2:]
        + taps[:, 1] * extended[:, 1:-1]
        + taps[:, 2] * extended[:, :-2]
    )
    gate_in = (filtered[1] * filtered[2]).astype(jnp.bfloat16)
    by_channel = lax.all_to_all(gate_in.T, "ctx", split_axis=0, concat_axis=1, tiled=True)
    length = by_channel.shape[1]
    signal = by_channel.astype(jnp.float32)
    kernel = long_filter(decay_rates, residues, length)
    sig_re, sig_im = forward_dft(signal)
    ker_re, ker_im = forward_dft(kernel)
    prod_re = sig_re * ker_re - sig_im * ker_im
    prod_im = sig_re * ker_im + sig_im * ker_re
    convolved = inverse_dft(prod_re, prod_im, length)
    long_out = (convolved + skip_gain[:, None] * signal).astype(jnp.bfloat16)
    returned = lax.all_to_all(long_out, "ctx", split_axis=1, concat_axis=0, tiled=True)
    gated = (filtered[0] * returned.T.astype(jnp.float32)).astype(jnp.bfloat16)
    partial_sum = (
        jnp.dot(
            gated,
            lax.all_gather(out_weight, "ctx", axis=1, tiled=True),
            preferred_element_type=jnp.float32,
        )
        .astype(jnp.bfloat16)
        .astype(jnp.float32)
    )
    summed = lax.psum(partial_sum.astype(jnp.bfloat16), "tp").astype(jnp.float32)
    kept = lax.dynamic_slice_in_dim(summed, tp_start, width_local, 1)
    return kept.astype(jnp.bfloat16)


def solution(mesh):
    in_specs = (
        P(None, "ctx", "tp"),
        P(),
        P(None, ("tp", "ctx")),
        P(None, ("tp", "ctx")),
        P(("tp", "ctx")),
        P("tp", "ctx"),
    )
    out_specs = P("ctx", "tp")
    return jax.shard_map(
        per_device, mesh=mesh, in_specs=in_specs, out_specs=out_specs, check_vma=False
    )
```

profile of v0, /device:TPU:4, one launch (start us, length us, event | category | flops | bytes accessed | tf_op | source)
XLA Modules:
  0.0 274.4 jit_solution(14337545069532780381)
XLA Ops:
  7.3 1.4 slice.31
  8.7 1.9 collective-permute-start
  10.6 15.2 %while.14 = (s32[]{:T(128)}, f32[32,4096]{1,0:T(8,128)S(1)}, f32[16,32]{1,0:T(8,128)}, f32[16,32]{1,0:T(8,128)}, s32[]{:T(128)}, /*index=5*/s32[]{:T(128)}) while((s32[]{:T(128)}, f32[32,4096]{1,0:T(8,128)S(1)}, f32[16,32]{1,0:T(8,128)}, f32[16,32]{1,0:T(8,128)}, s32[]{:T(128)}, /*index=5*/s32[]{:T(128)}) %tuple.41), condition=%wide.region_1.0_spmd.clone, body=%wide.region_0.0_spmd.clone.sunk | while | flops 524387 | bytes 1049427 | solution.py:87
  27.1 1.0 convolution_negate_fusion.1
  28.1 1.0 fusion.56
  29.9 0.8 convolution_subtract_fusion.2
  31.2 2.3 copy.28
  33.5 1.3 copy.48
  34.8 2.0 copy.27
  36.8 2.0 maximum_convert_fusion
  38.8 2.4 fusion.5
  41.2 1.2 copy-done.1
  42.4 0.8 fusion.16
  43.1 12.4 %all-to-all-start = ((bf16[32,32,128]{2,1,0:T(8,128)(2,1)}), bf16[32,32,128]{2,1,0:T(8,128)(2,1)}, u32[]{:S(2)}, u32[]{:S(2)}) async-start(bf16[32,32,128]{2,1,0:T(8,128)(2,1)} %bitcast.90), calls=%async_computation | async-start | bytes 524288 | tf_op jit(solution)/shard_map/all_to_all | solution.py:105
  55.8 1.6 fusion.26
  57.4 0.8 fusion.102
  58.1 1.7 convolution_add_fusion.1
  59.9 8.3 %all-to-all-done = bf16[32,32,128]{2,1,0:T(8,128)(2,1)} async-done(((bf16[32,32,128]{2,1,0:T(8,128)(2,1)}), bf16[32,32,128]{2,1,0:T(8,128)(2,1)}, u32[]{:S(2)}, u32[]{:S(2)}) %all-to-all-start) | async-done | bytes 262176 | tf_op jit(solution)/shard_map/all_to_all | solution.py:105
  68.2 1.1 copy.29
  70.7 0.7 fusion.25
  71.5 0.7 fusion.24
  72.2 0.8 convolution_add_fusion.2
  73.5 1.1 multiply_add_fusion
  77.5 1.7 fusion.12
  79.2 1.7 fusion.8
  81.6 1.5 fusion.19
  83.1 20.5 %all_to_all.26 = bf16[32,32,128]{2,0,1:T(8,128)(2,1)S(1)} all-to-all(bf16[32,32,128]{2,0,1:T(8,128)(2,1)S(1)} %fusion.19), channel_id=1, replica_groups=mesh['ctx'=32,'tp'=8] {'ctx'}, dimensions={1} | all-to-all | bytes 524288 | tf_op jit(solution)/shard_map/all_to_all | solution.py:115
  103.6 1.1 fusion.18
  104.7 66.7 %all-gather.2.cloned.1.call-done = bf16[1024,8192]{1,0:T(8,128)(2,1)} async-done(((bf16[1024,256]{1,0:T(8,128)(2,1)}), bf16[1024,8192]{1,0:T(8,128)(2,1)}) %all-gather.2.cloned.1.call-update) | async-done | bytes 16777232 | tf_op jit(solution)/shard_map/all_gather | solution.py:120
  171.4 9.6 %convolution_convert_fusion = bf16[128,8192]{1,0:T(8,128)(2,1)} fusion(bf16[128,1024]{0,1:T(8,128)(2,1)S(1)} %fusion.18, bf16[1024,8192]{1,0:T(8,128)(2,1)} %all-gather.2.cloned.1.call-done), kind=kOutput, calls=%fused_computation.8 | convolution fusion | flops 2148532224 | bytes 19136512 | tf_op jit(solution)/shard_map/dot_general | solution.py:118
  181.0 84.9 %all-reduce.2.cloned.1.call-done = bf16[128,8192]{1,0:T(8,128)(2,1)} async-done(((bf16[128,8192]{1,0:T(8,128)(2,1)}), bf16[128,8192]{1,0:T(8,128)(2,1)}) %all-reduce.2.cloned.1.call-update) | async-done | bytes 2097168 | tf_op jit(solution)/shard_map/psum | solution.py:126
  265.9 1.7 convert_convert_fusion
  (79 shorter events, 23.8 us)
Async XLA Ops:
  6.5 19.7 %copy-start = (f32[3,3,8192]{2,1,0:T(4,128)S(1)}, f32[3,3,8192]{2,1,0:T(4,128)}, u32[]{:S(2)}) copy-start(f32[3,3,8192]{2,1,0:T(4,128)} %param.9) | copy-start | bytes 884740
  6.5 164.9 %all-gather.2.cloned.1.call-start = ((), (), s32[]{:S(2)}) async-start(), calls=%async_computation.2 | async-start | bytes 17301504 | tf_op jit(solution)/shard_map/all_gather | solution.py:120
  8.7 26.2 %collective-permute-start = (bf16[3,2,1024]{2,1,0:T(2,128)(2,1)}, bf16[3,2,1024]{2,1,0:T(2,128)(2,1)}, u32[]{:S(2)}, u32[]{:S(2)}) collective-permute-start(bf16[3,2,1024]{2,1,0:T(2,128)(2,1)} %slice.31), channel_id=1, source_target_pairs={{0,8},{8,16},{16,24},{24,32},{32,40},{40,48},{48,56},{56,64},{64,7... | collective-permute-start | bytes 36872 | tf_op jit(solution)/shard_map/ppermute | solution.py:11
  26.4 3.4 %copy-start.6 = (f32[64,128]{1,0:T(8,128)}, f32[64,128]{1,0:T(8,128)S(1)}, u32[]{:S(2)}) copy-start(f32[64,128]{1,0:T(8,128)S(1)} %get-tuple-element.135) | copy-start | bytes 98308
  26.4 4.2 %copy-start.3 = (f32[64,128]{1,0:T(8,128)}, f32[64,128]{1,0:T(8,128)S(1)}, u32[]{:S(2)}) copy-start(f32[64,128]{1,0:T(8,128)S(1)} %get-tuple-element.134) | copy-start | bytes 98308
  36.8 2.0 copy-start.11
  36.8 2.0 copy-start.12
  41.2 1.2 copy-start.1
  43.1 25.0 %all-to-all-start = ((bf16[32,32,128]{2,1,0:T(8,128)(2,1)}), bf16[32,32,128]{2,1,0:T(8,128)(2,1)}, u32[]{:S(2)}, u32[]{:S(2)}) async-start(bf16[32,32,128]{2,1,0:T(8,128)(2,1)} %bitcast.90), calls=%async_computation | async-start | bytes 524288 | tf_op jit(solution)/shard_map/all_to_all | solution.py:105
  55.5 210.4 %all-reduce.2.cloned.1.call-start = ((), (), s32[]{:S(2)}) async-start(), calls=%async_computation.3 | async-start | bytes 4194304 | tf_op jit(solution)/shard_map/psum | solution.py:126
  55.8 2.4 copy-start.4
  55.8 2.4 copy-start.7
  69.5 1.2 copy-start.5
  69.5 1.2 copy-start.8
  72.2 1.2 copy-start.2
  76.7 0.8 copy-start.9
  76.7 0.8 copy-start.10
  80.9 0.7 copy-start.13
Sparse Core Ops, SparseCore 0:
  9.9 161.4 all-gather.1
  181.1 84.7 all-reduce.1
where the time goes:
time: 276 us; the launch traced here: 274 us
  waiting for transfers between devices  161 us (58%)
  matrix products  27.2 us (10%)
  other arithmetic  25.1 us (9%)
  blocking collectives  20.5 us (7%)
  starting transfers between devices  14.5 us (5%)
  between operations  13.8 us (5%)
  local copies, waits for them, and re-layouts  12.3 us (4%)
    psum x1, waiting for transfers between devices, per_device(): lax.psum(partial_sum.astype(jnp.bfloat16), 'tp').astype(jnp.float32)  84.9 us
    all_gather x1, waiting for transfers between devices, per_device(): lax.all_gather(out_weight, 'ctx', axis=1, tiled=True)  66.7 us
    all_to_all x1, blocking collectives, per_device(): lax.all_to_all(long_out, 'ctx', split_axis=1, concat_axis=0, tiled=True)  20.5 us
    all_to_all x1, starting transfers between devices, per_device(): lax.all_to_all(gate_in.T, 'ctx', split_axis=0, concat_axis=1, tiled=True)  12.4 us
    mul x16, other arithmetic, add_mode(): weight_now * jnp.sqrt(2.0 * rate_now) * jnp.exp(-rate_now * steps_axis)  11.5 us
    dot_general x1, matrix products, per_device(): jnp.dot(gated, lax.all_gather(out_weight, 'ctx', axis=1, tiled=True), pre...  9.56 us
    all_to_all x1, waiting for transfers between devices, per_device(): lax.all_to_all(gate_in.T, 'ctx', split_axis=0, concat_axis=1, tiled=True)  8.31 us
    unnamed x31, local copies, waits for them, and re-layouts  6.34 us
  transfers between devices with their start and end apart: 4, of which 3 were waited for; matrix products, arithmetic and copies ran while one was open for 19% of the time, Pallas kernels for 0%

commit v1 on v0

--- a/solution.py
+++ b/solution.py
@@ -117,7 +117,9 @@
     partial_sum = (
         jnp.dot(
             gated,
-            lax.all_gather(out_weight, "ctx", axis=1, tiled=True),
+            jnp.concatenate(
+                lax.all_to_all(jnp.stack([out_weight] * lax.axis_size("ctx")), "ctx", 0, 0), axis=1
+            ),
             preferred_element_type=jnp.float32,
         )
         .astype(jnp.bfloat16)

time: 276 us -> 593 us (2.15)
  waiting for transfers between devices: 161 us -> 478 us
  blocking collectives: 20.5 us -> 0 us
  starting transfers between devices: 14.5 us -> 29.2 us
    all_to_all x0 -> x2, waiting for transfers between devices: none -> 379 us  [the longest x1 368 us: per_device(): lax.all_to_all(jnp.stack([out_weight] * lax.axis_size('ctx')), 'ctx', 0, 0)]
    all_gather x1 -> x0, waiting for transfers between devices: 66.7 us -> none  [per_device(): lax.all_gather(out_weight, 'ctx', axis=1, tiled=True)]
    all_to_all x1 -> x0, blocking collectives: 20.5 us -> none  [per_device(): lax.all_to_all(long_out, 'ctx', split_axis=1, concat_axis=0, tiled=True)]
    all_to_all x0 -> x2, starting transfers between devices: none -> 14.8 us  [the longest x1 8.05 us: per_device(): lax.all_to_all(jnp.stack([out_weight] * lax.axis_size('ctx')), 'ctx', 0, 0)]
    another operation x0 -> x1, local copies, waits for them, and re-layouts: none -> 6.01 us  [per_device(): jnp.stack([out_weight] * lax.axis_size('ctx'))]
  transfers between devices with their start and end apart: 4 -> 5, of which waited for: 3 -> 4; matrix products, arithmetic and copies ran while one was open for 19% -> 5% of each run, Pallas kernels for 0% -> 0%
where the time goes in v1:
time: 593 us; the launch traced here: 591 us
  waiting for transfers between devices  478 us (81%)
  matrix products  31.2 us (5%)
  starting transfers between devices  29.2 us (5%)
  other arithmetic  24.9 us (4%)
  local copies, waits for them, and re-layouts  14 us (2%)
  between operations  13.7 us (2%)
    all_to_all x1, waiting for transfers between devices, per_device(): lax.all_to_all(jnp.stack([out_weight] * lax.axis_size('ctx')), 'ctx', 0, 0)  368 us
    psum x1, waiting for transfers between devices, per_device(): lax.psum(partial_sum.astype(jnp.bfloat16), 'tp').astype(jnp.float32)  90 us
    dot_general x1, matrix products, per_device(): jnp.dot(gated, jnp.concatenate(lax.all_to_all(jnp.stack([out_weight] * la...  12.8 us
    all_to_all x1, starting transfers between devices, per_device(): lax.all_to_all(gate_in.T, 'ctx', split_axis=0, concat_axis=1, tiled=True)  12.5 us
  transfers between devices with their start and end apart: 5, of which 4 were waited for; matrix products, arithmetic and copies ran while one was open for 5% of the time, Pallas kernels for 0%

profile of v1, /device:TPU:4, one launch (start us, length us, event | category | flops | bytes accessed | tf_op | source)
XLA Modules:
  0.0 591.4 jit_solution(10960782779868109835)
XLA Ops:
  6.5 0.9 slice.31
  7.4 1.9 collective-permute-start
  9.3 0.8 fusion.94
  10.1 15.2 %while.14 = (s32[]{:T(128)}, f32[32,4096]{1,0:T(8,128)S(1)}, f32[16,32]{1,0:T(8,128)}, f32[16,32]{1,0:T(8,128)}, s32[]{:T(128)}, /*index=5*/s32[]{:T(128)}) while((s32[]{:T(128)}, f32[32,4096]{1,0:T(8,128)S(1)}, f32[16,32]{1,0:T(8,128)}, f32[16,32]{1,0:T(8,128)}, s32[]{:T(128)}, /*index=5*/s32[]{:T(128)}) %tuple.41), condition=%wide.region_1.0_spmd.clone, body=%wide.region_0.0_spmd.clone.sunk | while | flops 524387 | bytes 1049435 | solution.py:87
  25.8 1.0 convolution_negate_fusion.1
  26.8 1.0 fusion.56
  27.9 1.5 fusion.27
  29.4 1.5 convolution_subtract_fusion.2
  30.9 2.3 copy.30
  33.3 2.0 copy.29
  35.2 2.0 maximum_convert_fusion
  37.2 2.4 fusion.5
  39.6 1.1 copy-done.2
  40.7 0.8 fusion.16
  41.5 12.5 %all-to-all-start = ((bf16[32,32,128]{2,1,0:T(8,128)(2,1)}), bf16[32,32,128]{2,1,0:T(8,128)(2,1)S(1)}, u32[]{:S(2)}, u32[]{:S(2)}) async-start(bf16[32,32,128]{2,1,0:T(8,128)(2,1)} %bitcast.94), calls=%async_computation | async-start | bytes 524288 | tf_op jit(solution)/shard_map/all_to_all | solution.py:105
  54.9 1.8 convolution_add_fusion.1
  56.6 9.0 %all-to-all-done = bf16[32,32,128]{2,1,0:T(8,128)(2,1)S(1)} async-done(((bf16[32,32,128]{2,1,0:T(8,128)(2,1)}), bf16[32,32,128]{2,1,0:T(8,128)(2,1)S(1)}, u32[]{:S(2)}, u32[]{:S(2)}) %all-to-all-start) | async-done | bytes 262176 | tf_op jit(solution)/shard_map/all_to_all | solution.py:105
  67.9 0.7 fusion.24
  69.9 1.1 multiply_add_fusion
  72.4 0.8 convolution_add_fusion
  73.9 1.7 fusion.12
  75.6 1.7 fusion.8
  77.6 1.3 fusion.19
  78.8 6.7 %all-to-all-start.1 = ((bf16[32,32,128]{2,0,1:T(8,128)(2,1)}), bf16[32,32,128]{2,0,1:T(8,128)(2,1)S(1)}, u32[]{:S(2)}, u32[]{:S(2)}) async-start(bf16[32,32,128]{2,0,1:T(8,128)(2,1)} %fusion.19), calls=%async_computation.1 | async-start | bytes 524288 | tf_op jit(solution)/shard_map/all_to_all | solution.py:115
  85.8 11.5 %all-to-all-done.1 = bf16[32,32,128]{2,0,1:T(8,128)(2,1)S(1)} async-done(((bf16[32,32,128]{2,0,1:T(8,128)(2,1)}), bf16[32,32,128]{2,0,1:T(8,128)(2,1)S(1)}, u32[]{:S(2)}, u32[]{:S(2)}) %all-to-all-start.1) | async-done | bytes 262176 | tf_op jit(solution)/shard_map/all_to_all | solution.py:115
  97.3 6.0 %stack.2 = bf16[32,1024,256]{1,2,0:T(8,128)(2,1)} broadcast(bf16[1024,256]{0,1:T(8,128)(2,1)S(1)} %copy.37), dimensions={1,2} | broadcast | bytes 17301504 | tf_op jit(solution)/shard_map/stack | solution.py:121
  103.3 8.1 %all-to-all-start.2 = ((bf16[32,1024,256]{1,2,0:T(8,128)(2,1)}), bf16[32,1024,256]{1,2,0:T(8,128)(2,1)}, u32[]{:S(2)}, u32[]{:S(2)}) async-start(bf16[32,1024,256]{1,2,0:T(8,128)(2,1)} %stack.2), calls=%async_computation.2 | async-start | bytes 33554432 | tf_op jit(solution)/shard_map/all_to_all | solution.py:121
  111.4 1.1 fusion.18
  112.5 367.5 %all-to-all-done.2 = bf16[32,1024,256]{1,2,0:T(8,128)(2,1)} async-done(((bf16[32,1024,256]{1,2,0:T(8,128)(2,1)}), bf16[32,1024,256]{1,2,0:T(8,128)(2,1)}, u32[]{:S(2)}, u32[]{:S(2)}) %all-to-all-start.2) | async-done | bytes 16777248 | tf_op jit(solution)/shard_map/all_to_all | solution.py:121
  480.0 12.8 %convolution_convert_fusion = bf16[128,8192]{1,0:T(8,128)(2,1)} fusion(bf16[128,1024]{0,1:T(8,128)(2,1)S(1)} %fusion.18, bf16[1024,8192]{0,1:T(8,128)(2,1)} %bitcast.17), kind=kOutput, calls=%fused_computation.8 | convolution fusion | flops 2148532224 | bytes 19136512 | tf_op jit(solution)/shard_map/dot_general | solution.py:118
  492.9 90.0 %all-reduce.2.cloned.1.call-done = bf16[128,8192]{1,0:T(8,128)(2,1)} async-done(((bf16[128,8192]{1,0:T(8,128)(2,1)}), bf16[128,8192]{1,0:T(8,128)(2,1)}) %all-reduce.2.cloned.1.call-update) | async-done | bytes 2097168 | tf_op jit(solution)/shard_map/psum | solution.py:128
  582.9 1.7 convert_convert_fusion
  (69 shorter events, 22.3 us)
Async XLA Ops:
  6.5 21.3 %copy-start = (f32[3,3,8192]{2,1,0:T(4,128)S(1)}, f32[3,3,8192]{2,1,0:T(4,128)}, u32[]{:S(2)}) copy-start(f32[3,3,8192]{2,1,0:T(4,128)} %param.9) | copy-start | bytes 884740
  7.4 25.8 %collective-permute-start = (bf16[3,2,1024]{2,1,0:T(2,128)(2,1)S(1)}, bf16[3,2,1024]{2,1,0:T(2,128)(2,1)}, u32[]{:S(2)}, u32[]{:S(2)}) collective-permute-start(bf16[3,2,1024]{2,1,0:T(2,128)(2,1)S(1)} %slice.31), channel_id=1, source_target_pairs={{0,8},{8,16},{16,24},{24,32},{32,40},{40,48},{48,56},{56,64},{64,7... | collective-permute-start | bytes 36872 | tf_op jit(solution)/shard_map/ppermute | solution.py:11
  37.2 16.8 %copy-start.4 = (f32[64,128]{1,0:T(8,128)S(1)}, f32[64,128]{1,0:T(8,128)}, u32[]{:S(2)}) copy-start(f32[64,128]{1,0:T(8,128)} %get-tuple-element.134) | copy-start | bytes 98308
  37.2 16.8 %copy-start.5 = (f32[64,128]{1,0:T(8,128)S(1)}, f32[64,128]{1,0:T(8,128)}, u32[]{:S(2)}) copy-start(f32[64,128]{1,0:T(8,128)} %get-tuple-element.135) | copy-start | bytes 98308
  39.6 1.1 copy-start.2
  41.5 24.1 %all-to-all-start = ((bf16[32,32,128]{2,1,0:T(8,128)(2,1)}), bf16[32,32,128]{2,1,0:T(8,128)(2,1)S(1)}, u32[]{:S(2)}, u32[]{:S(2)}) async-start(bf16[32,32,128]{2,1,0:T(8,128)(2,1)} %bitcast.94), calls=%async_computation | async-start | bytes 524288 | tf_op jit(solution)/shard_map/all_to_all | solution.py:105
  68.7 1.2 copy-start.3
  75.6 1.9 copy-start.7
  77.3 8.2 %copy-start.6 = (bf16[1024,256]{1,0:T(8,128)(2,1)S(1)}, bf16[1024,256]{1,0:T(8,128)(2,1)}, u32[]{:S(2)}) copy-start(bf16[1024,256]{1,0:T(8,128)(2,1)} %param.13) | copy-start | bytes 1572868
  78.8 18.5 %all-to-all-start.1 = ((bf16[32,32,128]{2,0,1:T(8,128)(2,1)}), bf16[32,32,128]{2,0,1:T(8,128)(2,1)S(1)}, u32[]{:S(2)}, u32[]{:S(2)}) async-start(bf16[32,32,128]{2,0,1:T(8,128)(2,1)} %fusion.19), calls=%async_computation.1 | async-start | bytes 524288 | tf_op jit(solution)/shard_map/all_to_all | solution.py:115
  103.3 376.7 %all-to-all-start.2 = ((bf16[32,1024,256]{1,2,0:T(8,128)(2,1)}), bf16[32,1024,256]{1,2,0:T(8,128)(2,1)}, u32[]{:S(2)}, u32[]{:S(2)}) async-start(bf16[32,1024,256]{1,2,0:T(8,128)(2,1)} %stack.2), calls=%async_computation.2 | async-start | bytes 33554432 | tf_op jit(solution)/shard_map/all_to_all | solution.py:121
  111.4 471.5 %all-reduce.2.cloned.1.call-start = ((), (), s32[]{:S(2)}) async-start(), calls=%async_computation.3 | async-start | bytes 4194304 | tf_op jit(solution)/shard_map/psum | solution.py:128
  480.0 104.5 %copy-start.1 = (f32[3,3,8192]{2,1,0:T(4,128)S(1)}, f32[3,3,8192]{2,1,0:T(4,128)}, u32[]{:S(2)}) copy-start(f32[3,3,8192]{2,1,0:T(4,128)} %param.9) | copy-start | bytes 884740
Sparse Core Ops, SparseCore 0:
  493.0 89.8 all-reduce.1
